TPU v7x, 1024 devices: a whole 8x8x8 slice. The times are simulated.
1024 devices in a mesh: grp: 8 (over z), exp: 16 (over y, core), rep: 8 (over x).
Axes of the slice: x: 8, y: 8, z: 8, core: 2. Of those that a mesh axis runs over, the one named last changes fastest.
Arguments:
- tokens: bfloat16 [16384, 2048], P(('rep', 'grp', 'exp')), parts along dimension 0, may hold values from -6 to 6
- expert_ids: int32 [16384, 8], P(('rep', 'grp', 'exp')), parts along dimension 0, may hold values from 0 to 127, as said below
- gate_weights: bfloat16 [16384, 8], P(('rep', 'grp', 'exp')), parts along dimension 0, may hold values from 0.049804688 to 0.3984375
- w_gate: bfloat16 [128, 2048, 768], P(('grp', 'exp')), may hold values from -0.125 to 0.125
- w_up: bfloat16 [128, 2048, 768], P(('grp', 'exp')), may hold values from -0.125 to 0.125
- w_down: bfloat16 [128, 768, 2048], P(('grp', 'exp')), may hold values from -0.21875 to 0.21875
Outputs:
- combined: float32 [16384, 2048], P(('rep', 'grp', 'exp')), parts along dimension 0
There are 8 independent parts, one for each index of `rep`. A program takes and returns all parts, laid end to end along the dimension named above; an argument that names none is the same for every part. Nothing has to cross between parts.
Inputs may be any that keep to these rules, and one draw needn't show every extreme that they name: `expert_ids`: expert x belongs to group x // 16. Each row names 8 different experts, 4 of them in each of two different groups. Of the 16 rows of one device (aligned blocks of 16 rows), at most 8 name experts of any one group and at most 2 name any one expert; in every draw one group is named by 8 rows of every device, and each of its experts by 2 rows of every device.
All inputs are finite; a program needn't handle non-finite values.
Results may differ from a plain program's by a relative error of at most 0.0041.
Values may be sent and summed in bfloat16 or wider, within the bound.
A program may use at most 32 MiB of HBM per device.

v0:
```python
import jax
import jax.numpy as jnp
from jax import lax
from jax.sharding import PartitionSpec as P


def expert_apply(token_rows, gate_mat, up_mat, down_mat):
    gate_pre = jnp.dot(token_rows, gate_mat, preferred_element_type=jnp.float32)
    up_pre = jnp.dot(token_rows, up_mat, preferred_element_type=jnp.float32)
    hidden = (jax.nn.silu(gate_pre) * up_pre).astype(jnp.bfloat16)
    return jnp.dot(hidden, down_mat, preferred_element_type=jnp.float32).astype(jnp.bfloat16)


def shards(tokens, expert_ids, gate_weights, w_gate, w_up, w_down):
    tok_rows, model_width = tokens.shape
    top_count = expert_ids.shape[1]
    groups = lax.axis_size("grp")
    owners = lax.axis_size("exp")
    experts = groups * owners
    cap_group = 4 * tok_rows // groups
    cap_expert = cap_group * (top_count // 2) // owners
    gate_mat = w_gate[0]
    up_mat = w_up[0]
    down_mat = w_down[0]
    gate_values = gate_weights.astype(jnp.float32)
    zero_gate = jnp.zeros((), jnp.bfloat16)
    expert_grid = jnp.arange(experts, dtype=jnp.int32)
    chosen = (expert_ids[:, :, None] == expert_grid).astype(jnp.int32)
    per_token = jnp.sum(chosen, axis=1)
    earlier = jnp.cumsum(per_token, axis=0) - per_token
    slot_rank = jnp.sum(chosen * earlier[:, None, :], axis=2)
    slot_grid = jnp.arange(cap_expert, dtype=jnp.int32)
    group_of = expert_ids // owners
    group_grid = jnp.arange(groups, dtype=jnp.int32)
    touched = jnp.any(group_of[:, :, None] == group_grid, axis=1).astype(jnp.int32)
    group_rank = jnp.cumsum(touched, axis=0) - touched
    row_grid = jnp.arange(cap_group, dtype=jnp.int32)
    placing = (group_rank.T[:, :, None] == row_grid) & (touched.T[:, :, None] > 0)
    place_count = placing.astype(jnp.int32)
    slot_table = jnp.sum(chosen * (slot_rank[:, :, None] + 1), axis=1).reshape(
        tok_rows, groups, owners
    )
    gate_table = jnp.sum(jnp.where(chosen > 0, gate_values[:, :, None], 0.0), axis=1).reshape(
        tok_rows, groups, owners
    )
    outgoing = jnp.einsum(
        "gtc,td->gcd", placing.astype(jnp.bfloat16), tokens, preferred_element_type=jnp.float32
    ).astype(jnp.bfloat16)
    sent_slots = jnp.einsum("gtc,tge->gce", place_count, slot_table) - 1
    sent_gates = jnp.einsum(
        "gtc,tge->gce", placing.astype(jnp.float32), gate_table, precision=lax.Precision.HIGHEST
    ).astype(jnp.bfloat16)
    arrived, arrived_slots, arrived_gates = (
        lax.all_to_all(outgoing, "grp", split_axis=0, concat_axis=0, tiled=True),
        lax.all_to_all(sent_slots, "grp", split_axis=0, concat_axis=0, tiled=True),
        lax.all_to_all(sent_gates, "grp", split_axis=0, concat_axis=0, tiled=True),
    )
    spread = (
        jnp.transpose(arrived_slots, (0, 2, 1))[:, :, None, :] == slot_grid[None, None, :, None]
    )
    buffer = jnp.einsum(
        "gesc,gcd->gesd", spread.astype(jnp.bfloat16), arrived, preferred_element_type=jnp.float32
    ).astype(jnp.bfloat16)
    pieces = lax.all_to_all(buffer, "exp", split_axis=1, concat_axis=0, tiled=True)
    layout = pieces.shape
    result = expert_apply(pieces.reshape(-1, model_width), gate_mat, up_mat, down_mat)
    computed = result.reshape(layout)
    returned = lax.all_to_all(computed, "exp", split_axis=0, concat_axis=1, tiled=True)
    gate_lookup = jnp.transpose(arrived_gates, (0, 2, 1))[:, :, None, :]
    weighting = jnp.where(spread, gate_lookup, zero_gate)
    partial_sums = jnp.einsum(
        "gesc,gesd->gcd", weighting, returned, preferred_element_type=jnp.float32
    )
    at_owner = lax.all_to_all(partial_sums, "grp", split_axis=0, concat_axis=0, tiled=True)
    return jnp.einsum(
        "gtc,gcd->td", placing.astype(jnp.float32), at_owner, precision=lax.Precision.HIGHEST
    )


def solution(mesh):
    return jax.shard_map(
        shards,
        mesh=mesh,
        in_specs=(
            P(("rep", "grp", "exp"), None),
            P(("rep", "grp", "exp"), None),
            P(("rep", "grp", "exp"), None),
            P(("grp", "exp"), None, None),
            P(("grp", "exp"), None, None),
            P(("grp", "exp"), None, None),
        ),
        out_specs=P(("rep", "grp", "exp"), None),
        check_vma=False,
    )
```

profile of v0, /device:TPU:1, one launch (start us, length us, event | category | flops | bytes accessed | tf_op | source)
XLA Modules:
  0.0 156.8 jit_solution(17813048514218991013)
XLA Ops:
  0.0 0.9 copy.60
  1.1 0.4 select_reduce_fusion.2
  2.3 0.7 reshape.42
  3.0 17.2 %all-to-all-start = ((s32[8,1,128]{2,1,0:T(1,128)}), s32[8,1,128]{2,1,0:T(1,128)S(1)}, u32[]{:S(2)}, u32[]{:S(2)}) async-start(s32[8,1,128]{2,1,0:T(1,128)} %reshape.42), calls=%async_computation | async-start | bytes 8192 | tf_op jit(solution)/shard_map/all_to_all | solution.py:55
  20.2 1.7 %convolution_convert_fusion.1 = bf16[8,8,2048]{2,1,0:T(8,128)(2,1)} fusion(bf16[16,2048]{1,0:T(8,128)(2,1)} %param.6, pred[8,16,8]{1,0,2:T(8,128)(4,1)S(1)} %fusion.30), kind=kOutput, calls=%fused_computation.9 | convolution fusion | flops 4325376 | bytes 328704 | tf_op jit(solution)/shard_map/gtc,td->gcd/dot_general | solution.py:46
  21.9 4.7 %all-to-all-done = s32[8,1,128]{2,1,0:T(1,128)S(1)} async-done(((s32[8,1,128]{2,1,0:T(1,128)}), s32[8,1,128]{2,1,0:T(1,128)S(1)}, u32[]{:S(2)}, u32[]{:S(2)}) %all-to-all-start) | async-done | bytes 4128 | tf_op jit(solution)/shard_map/all_to_all | solution.py:55
  26.7 3.4 %all-to-all-start.2 = ((bf16[8,8,2048]{2,1,0:T(8,128)(2,1)}), bf16[8,8,2048]{2,1,0:T(8,128)(2,1)S(1)}, u32[]{:S(2)}, u32[]{:S(2)}) async-start(bf16[8,8,2048]{2,1,0:T(8,128)(2,1)} %convolution_convert_fusion.1), calls=%async_computation.2 | async-start | bytes 524288 | tf_op jit(solution)/shard_map/all_to_all | solution.py:54
  30.1 0.5 broadcast.44
  30.6 0.7 reduce
  31.3 8.0 %all-to-all-done.2 = bf16[8,8,2048]{2,1,0:T(8,128)(2,1)S(1)} async-done(((bf16[8,8,2048]{2,1,0:T(8,128)(2,1)}), bf16[8,8,2048]{2,1,0:T(8,128)(2,1)S(1)}, u32[]{:S(2)}, u32[]{:S(2)}) %all-to-all-start.2) | async-done | bytes 262176 | tf_op jit(solution)/shard_map/all_to_all | solution.py:54
  39.3 0.5 convolution_convert_fusion
  39.8 2.1 %copy.75 = bf16[8,16,2,2048]{3,2,0,1:T(2,128)(2,1)} copy(bf16[8,16,2,2048]{3,1,2,0:T(8,128)(2,1)S(1)} %convolution_convert_fusion) | data formatting | bytes 2097152 | tf_op jit(solution)/shard_map/convert_element_type | solution.py:63
  41.8 11.1 %all-to-all-start.3 = ((bf16[8,16,2,2048]{3,2,0,1:T(2,128)(2,1)}), bf16[8,16,2,2048]{3,2,0,1:T(2,128)(2,1)}, u32[]{:S(2)}, u32[]{:S(2)}) async-start(bf16[8,16,2,2048]{3,2,0,1:T(2,128)(2,1)} %copy.75), calls=%async_computation.3 | async-start | bytes 2097152 | tf_op jit(solution)/shard_map/all_to_all | solution.py:64
  53.2 0.8 convolution_convert_fusion.2
  54.0 27.0 %all-to-all-done.3 = bf16[8,16,2,2048]{3,2,0,1:T(2,128)(2,1)} async-done(((bf16[8,16,2,2048]{3,2,0,1:T(2,128)(2,1)}), bf16[8,16,2,2048]{3,2,0,1:T(2,128)(2,1)}, u32[]{:S(2)}, u32[]{:S(2)}) %all-to-all-start.3) | async-done | bytes 1048608 | tf_op jit(solution)/shard_map/all_to_all | solution.py:64
  81.0 3.3 %all-to-all-start.1 = ((bf16[8,8,16]{2,1,0:T(8,128)(2,1)}), bf16[8,8,16]{2,1,0:T(8,128)(2,1)S(1)}, u32[]{:S(2)}, u32[]{:S(2)}) async-start(bf16[8,8,16]{2,1,0:T(8,128)(2,1)} %convolution_convert_fusion.2), calls=%async_computation.1 | async-start | bytes 32768 | tf_op jit(solution)/shard_map/all_to_all | solution.py:56
  84.4 2.3 %reshape.36 = bf16[256,2048]{1,0:T(8,128)(2,1)} reshape(bf16[16,8,1,2,2048]{4,3,1,0,2:T(2,128)(2,1)} %bitcast.8) | data formatting | bytes 2097152 | tf_op jit(solution)/shard_map/reshape | solution.py:66
  86.6 4.1 %fusion.4 = f32[256,768]{1,0:T(8,128)} fusion(bf16[256,2048]{1,0:T(8,128)(2,1)} %reshape.36, bf16[1,2048,768]{2,1,0:T(8,128)(2,1)} %param.9), kind=kOutput, calls=%fused_computation.4 | convolution fusion | flops 805306368 | bytes 4980736 | tf_op jit(solution)/shard_map/dot_general | solution.py:8
  90.7 5.6 %fusion.6 = bf16[256,2048]{1,0:T(8,128)(2,1)} fusion(bf16[1,768,2048]{2,1,0:T(8,128)(2,1)S(1)} %copy-done, bf16[256,2048]{1,0:T(8,128)(2,1)} %reshape.36, bf16[1,2048,768]{2,1,0:T(8,128)(2,1)} %param.10, f32[256,768]{1,0:T(8,128)} %fusion.4), kind=kOutput, calls=%fused_computation.6 | convolution fusion | flops 1612316672 | bytes 9175040 | tf_op jit(solution)/shard_map/dot_general | solution.py:11
  96.3 2.5 %reshape.37 = bf16[128,1,2,2048]{3,2,0,1:T(2,128)(2,1)} reshape(bf16[256,2048]{1,0:T(8,128)(2,1)} %fusion.6) | data formatting | bytes 2097152 | tf_op jit(solution)/shard_map/reshape | solution.py:67
  98.8 31.8 %all_to_all.53 = bf16[128,1,2,2048]{3,2,1,0:T(2,128)(2,1)S(1)} all-to-all(bf16[128,1,2,2048]{3,2,1,0:T(2,128)(2,1)} %bitcast.50), channel_id=1, replica_groups=mesh['grp'=8,'exp'=16,'rep'=8] {'exp'}, dimensions={0} | all-to-all | bytes 2097152 | tf_op jit(solution)/shard_map/all_to_all | solution.py:68
  130.7 0.7 convolution_bitcast_fusion
  131.3 24.2 %all_to_all.54 = f32[8,8,2048]{2,1,0:T(8,128)S(1)} all-to-all(f32[8,8,2048]{2,1,0:T(8,128)S(1)} %convolution_bitcast_fusion), channel_id=1, replica_groups=mesh['grp'=8,'exp'=16,'rep'=8] {'grp'}, dimensions={0} | all-to-all | bytes 1048576 | tf_op jit(solution)/shard_map/all_to_all | solution.py:74
  155.6 1.2 convolution_bitcast_fusion.1
  (26 shorter events, 1.2 us)
Async XLA Ops:
  0.0 90.7 %copy-start = (bf16[1,768,2048]{2,1,0:T(8,128)(2,1)S(1)}, bf16[1,768,2048]{2,1,0:T(8,128)(2,1)}, u32[]{:S(2)}) copy-start(bf16[1,768,2048]{2,1,0:T(8,128)(2,1)} %param.11) | copy-start | bytes 9437188
  3.0 23.7 %all-to-all-start = ((s32[8,1,128]{2,1,0:T(1,128)}), s32[8,1,128]{2,1,0:T(1,128)S(1)}, u32[]{:S(2)}, u32[]{:S(2)}) async-start(s32[8,1,128]{2,1,0:T(1,128)} %reshape.42), calls=%async_computation | async-start | bytes 8192 | tf_op jit(solution)/shard_map/all_to_all | solution.py:55
  20.2 32.8 %copy-start.1 = (bf16[16,8]{0,1:T(8,128)(2,1)S(1)}, bf16[16,8]{0,1:T(8,128)(2,1)}, u32[]{:S(2)}) copy-start(bf16[16,8]{0,1:T(8,128)(2,1)} %param.8) | copy-start | bytes 772
  26.7 12.6 %all-to-all-start.2 = ((bf16[8,8,2048]{2,1,0:T(8,128)(2,1)}), bf16[8,8,2048]{2,1,0:T(8,128)(2,1)S(1)}, u32[]{:S(2)}, u32[]{:S(2)}) async-start(bf16[8,8,2048]{2,1,0:T(8,128)(2,1)} %convolution_convert_fusion.1), calls=%async_computation.2 | async-start | bytes 524288 | tf_op jit(solution)/shard_map/all_to_all | solution.py:54
  41.8 39.2 %all-to-all-start.3 = ((bf16[8,16,2,2048]{3,2,0,1:T(2,128)(2,1)}), bf16[8,16,2,2048]{3,2,0,1:T(2,128)(2,1)}, u32[]{:S(2)}, u32[]{:S(2)}) async-start(bf16[8,16,2,2048]{3,2,0,1:T(2,128)(2,1)} %copy.75), calls=%async_computation.3 | async-start | bytes 2097152 | tf_op jit(solution)/shard_map/all_to_all | solution.py:64
  81.0 17.8 %all-to-all-start.1 = ((bf16[8,8,16]{2,1,0:T(8,128)(2,1)}), bf16[8,8,16]{2,1,0:T(8,128)(2,1)S(1)}, u32[]{:S(2)}, u32[]{:S(2)}) async-start(bf16[8,8,16]{2,1,0:T(8,128)(2,1)} %convolution_convert_fusion.2), calls=%async_computation.1 | async-start | bytes 32768 | tf_op jit(solution)/shard_map/all_to_all | solution.py:56
where the time goes:
time: 157 us
  blocking collectives  56 us (36%)
  waiting for transfers between devices  39.7 us (25%)
  starting transfers between devices  35.1 us (22%)
  matrix products  14.7 us (9%)
  local copies, waits for them, and re-layouts  9.61 us (6%)
    all_to_all x1, blocking collectives, shards(): lax.all_to_all(computed, 'exp', split_axis=0, concat_axis=1, tiled=True)  31.8 us
    all_to_all x1, waiting for transfers between devices, shards(): lax.all_to_all(buffer, 'exp', split_axis=1, concat_axis=0, tiled=True)  27 us
    all_to_all x1, blocking collectives, shards(): lax.all_to_all(partial_sums, 'grp', split_axis=0, concat_axis=0, tiled=True)  24.2 us
    all_to_all x1, starting transfers between devices, shards(): lax.all_to_all(sent_slots, 'grp', split_axis=0, concat_axis=0, tiled=True)  17.2 us
    all_to_all x1, starting transfers between devices, shards(): lax.all_to_all(buffer, 'exp', split_axis=1, concat_axis=0, tiled=True)  11.1 us
    all_to_all x1, waiting for transfers between devices, shards(): lax.all_to_all(outgoing, 'grp', split_axis=0, concat_axis=0, tiled=True)  7.95 us
    dot_general x1, matrix products, expert_apply(): jnp.dot(hidden, down_mat, preferred_element_type=jnp.float32)  5.55 us
    all_to_all x1, waiting for transfers between devices, shards(): lax.all_to_all(sent_slots, 'grp', split_axis=0, concat_axis=0, tiled=True)  4.73 us
  transfers between devices with their start and end apart: 4, of which 3 were waited for; matrix products, arithmetic and copies ran while one was open for 12% of the time, Pallas kernels for 0%

commit v1 on v0

v1 whole, which is shorter than its diff:
```python
import functools
import jax
import jax.numpy as jnp
from jax import lax
from jax.experimental import pallas as pl
from jax.experimental.pallas import tpu as pltpu
from jax.sharding import PartitionSpec as P

F32 = jnp.float32
BF16 = jnp.bfloat16
STREAMS = 4
TILE = 256


def iota(shape, dim):
    return lax.broadcasted_iota(jnp.int32, shape, dim)


def dot(a, b):
    return jnp.dot(a, b, preferred_element_type=F32)


def dot_nt(a, b):
    return lax.dot_general(a, b, (((1,), (1,)), ((), ())), preferred_element_type=F32)


def kernel(
    ring,
    ids_ref, gates_ref, tok_ref, wg_hbm, wu_hbm, wd_hbm, o_ref,
    g_own, g_in, c_tab, s_tab, in1, out2, in2, out3, in3, out4, in4,
    wg, wu, wd, acc_g, acc_u, hid,
    w_sem, g_send, g_recv, send1, recv1, send2, recv2, send3, recv3, send4, recv4,
):
    toks, width = tok_ref.shape
    ff = wg.shape[1]
    blocks = 2 * ring
    rows2 = blocks * blocks
    rows1 = ring * toks
    experts = ring * blocks
    cols = width // STREAMS
    z = lax.axis_index("grp")
    e = lax.axis_index("exp")
    y = e // 2
    c = lax.rem(e, 2)

    def path_of(s):
        return s % 2

    def near(path, d):
        if path == 0:
            other = lax.rem(z + d, ring)
            return other, {"grp": other, "exp": e}
        other = lax.rem(y + d, ring)
        return other, {"grp": z, "exp": other * 2 + c}

    def near_me(path):
        return z if path == 0 else y

    def far(path, d, f):
        core = lax.rem(c + f, 2)
        if path == 0:
            other = lax.rem(y + d, ring) * 2 + core
            return other, {"grp": z, "exp": other}
        other = lax.rem(z + d, ring)
        return other * 2 + core, {"grp": other, "exp": y * 2 + core}

    def far_me(path):
        return e if path == 0 else z * 2 + c

    def distance(j):
        return ring // 2 + ((j + 1) // 2) * (1 - 2 * lax.rem(j, 2))

    def each_near(body):
        lax.fori_loop(0, ring - 1, lambda j, x: (body(distance(j)), x)[1], 0)

    def each_far(body):
        lax.fori_loop(
            0, 2 * (ring - 1), lambda j, x: (body(distance(j // 2), lax.rem(j, 2)), x)[1], 0
        )
        body(0, 1)

    def remote(src, dst, send, recv, device):
        return pltpu.make_async_remote_copy(
            src_ref=src, dst_ref=dst, send_sem=send, recv_sem=recv,
            device_id=device, device_id_type=pl.DeviceIdType.MESH,
        )

    def wait_bytes(ref, count, sem):
        part = ref.at[pl.ds(0, count)]
        pltpu.make_async_copy(part, part, sem).wait()

    loads = [
        pltpu.make_async_copy(hbm, vmem, w_sem.at[i])
        for i, (hbm, vmem) in enumerate(((wg_hbm, wg), (wu_hbm, wu), (wd_hbm, wd)))
    ]
    for load in loads:
        load.start()

    barrier = pltpu.get_barrier_semaphore()

    for path in range(2):
        def greet(d, f, path=path):
            pl.semaphore_signal(
                barrier, inc=1, device_id=far(path, d, f)[1],
                device_id_type=pl.DeviceIdType.MESH,
            )
        lax.fori_loop(
            0, 2 * (ring - 1), lambda j, x: (greet(distance(j // 2), lax.rem(j, 2)), x)[1], 0
        )
    greet(0, 1)

    table = jnp.zeros((toks, experts), F32)
    lane = iota((toks, experts), 1)
    for k in range(ids_ref.shape[1]):
        table = table + jnp.where(
            ids_ref[:, k:k + 1] == lane, gates_ref[:, k:k + 1].astype(F32), 0.0
        )
    table = table.astype(BF16)
    g_own[...] = table
    for path in range(2):
        g_in[path, near_me(path)] = table
    for s in range(STREAMS):
        in1[s, near_me(path_of(s))] = tok_ref[:, s * cols:(s + 1) * cols]

    pl.semaphore_wait(barrier, 4 * (ring - 1) + 1)

    for path in range(2):
        def send_table(d, path=path):
            remote(
                g_own, g_in.at[path, near_me(path)], g_send.at[path], g_recv.at[path],
                near(path, d)[1],
            ).start()
        each_near(send_table)
    for s in range(STREAMS):
        def send_rows(d, s=s, path=path_of(s)):
            remote(
                tok_ref.at[:, pl.ds(s * cols, cols)], in1.at[s, near_me(path)],
                send1.at[s], recv1.at[s], near(path, d)[1],
            ).start()
        each_near(send_rows)

    for path in range(2):
        wait_bytes(g_in.at[path], ring - 1, g_recv.at[path])
        gates = g_in[path].reshape(rows1, experts)
        named = jnp.where(gates.astype(F32) > 0, 1.0, 0.0).astype(BF16)
        r, q = iota((rows1, rows1), 0), iota((rows1, rows1), 1)
        below = jnp.where((r // toks == q // toks) & (q < r), 1.0, 0.0).astype(BF16)
        rank = dot(below, named).astype(BF16)

        def expert_of(slot, path=path):
            block = slot // blocks
            if path == 0:
                return z * blocks + block
            return (block // 2) * blocks + y * 2 + lax.rem(block, 2)

        pick = jnp.where(
            iota((experts, rows2), 0) == expert_of(iota((experts, rows2), 1)), 1.0, 0.0
        ).astype(BF16)
        row, slot = iota((rows1, rows2), 0), iota((rows1, rows2), 1)
        fits = (row // toks == lax.rem(slot // 2, ring)) & (
            dot(rank, pick) == lax.rem(slot, 2).astype(F32)
        )
        c_tab[path] = jnp.where(fits, dot(gates, pick), 0.0).astype(BF16)
        pick_t = jnp.where(
            iota((rows2, experts), 1) == expert_of(iota((rows2, experts), 0)), 1.0, 0.0
        ).astype(BF16)
        row, slot = iota((rows2, rows1), 1), iota((rows2, rows1), 0)
        fits = (row // toks == lax.rem(slot // 2, ring)) & (
            dot_nt(pick_t, rank) == lax.rem(slot, 2).astype(F32)
        )
        s_tab[path] = jnp.where(fits & (dot_nt(pick_t, gates) > 0), 1.0, 0.0).astype(BF16)

    for s in range(STREAMS):
        path = path_of(s)
        wait_bytes(in1.at[s], ring - 1, recv1.at[s])
        chosen = dot(s_tab[path], in1[s].reshape(rows1, cols)).astype(BF16)
        out2[s] = chosen.reshape(blocks, blocks, cols)
        in2[s, far_me(path)] = out2[s, far_me(path)]

        def send_chosen(d, f, s=s, path=path):
            to, device = far(path, d, f)
            remote(
                out2.at[s, to], in2.at[s, far_me(path)], send2.at[s], recv2.at[s], device
            ).start()
        each_far(send_chosen)

    r, q = iota((rows2, rows2), 0), iota((rows2, rows2), 1)
    swapped = (
        lax.rem(r // 2, ring) * (2 * blocks)
        + lax.rem(r // blocks, 2) * blocks
        + (r // (2 * blocks)) * 2
        + lax.rem(r, 2)
    )
    swap = jnp.where(q == swapped, 1.0, 0.0).astype(BF16)

    for s in range(STREAMS):
        wait_bytes(in2.at[s], blocks - 1, recv2.at[s])
        rows = in2[s].reshape(rows2, cols)
        if path_of(s) == 1:
            rows = dot(swap, rows).astype(BF16)
        if s == 0:
            loads[0].wait()
            loads[1].wait()

        def project(j, x, s=s, rows=rows):
            at = pl.ds(pl.multiple_of(j * TILE, TILE), TILE)
            gate_part = dot(rows, wg[s * cols:(s + 1) * cols, at])
            up_part = dot(rows, wu[s * cols:(s + 1) * cols, at])
            if s > 0:
                gate_part = gate_part + acc_g[:, at]
                up_part = up_part + acc_u[:, at]
            if s < STREAMS - 1:
                acc_g[:, at] = gate_part
                acc_u[:, at] = up_part
            else:
                hid[0, :, at] = (gate_part * jax.nn.sigmoid(gate_part) * up_part).astype(BF16)
            return x
        lax.fori_loop(0, ff // TILE, project, 0)
    hid[1] = dot(swap, hid[0]).astype(BF16)
    loads[2].wait()

    for s in range(STREAMS):
        path = path_of(s)
        hidden = hid[path]

        def down(j, x, s=s, hidden=hidden):
            at = pl.ds(pl.multiple_of(j * TILE, TILE), TILE)
            here = pl.ds(pl.multiple_of(s * cols + j * TILE, TILE), TILE)
            out3[s, :, :, at] = dot(hidden, wd[:, here]).astype(BF16).reshape(
                blocks, blocks, TILE
            )
            return x
        lax.fori_loop(0, cols // TILE, down, 0)
        in3[s, far_me(path)] = out3[s, far_me(path)]

        def send_back(d, f, s=s, path=path):
            to, device = far(path, d, f)
            remote(
                out3.at[s, to], in3.at[s, far_me(path)], send3.at[s], recv3.at[s], device
            ).start()
        each_far(send_back)

    for s in range(STREAMS):
        path = path_of(s)
        wait_bytes(in3.at[s], blocks - 1, recv3.at[s])
        summed = dot(c_tab[path], in3[s].reshape(rows2, cols)).astype(BF16)
        out4[s] = summed.reshape(ring, toks, cols)
        in4[s, near_me(path)] = out4[s, near_me(path)]

        def send_sum(d, s=s, path=path):
            to, device = near(path, d)
            remote(
                out4.at[s, to], in4.at[s, near_me(path)], send4.at[s], recv4.at[s], device
            ).start()
        each_near(send_sum)

    for s in range(STREAMS):
        wait_bytes(in4.at[s], ring - 1, recv4.at[s])
        total = in4[s, 0].astype(F32)
        for i in range(1, ring):
            total = total + in4[s, i].astype(F32)
        o_ref[:, s * cols:(s + 1) * cols] = total

    for path in range(2):
        wait_bytes(g_in.at[path], ring - 1, g_send.at[path])
    for s in range(STREAMS):
        wait_bytes(in1.at[s], ring - 1, send1.at[s])
        wait_bytes(out2.at[s], blocks - 1, send2.at[s])
        wait_bytes(out3.at[s], blocks - 1, send3.at[s])
        wait_bytes(out4.at[s], ring - 1, send4.at[s])


def shards(tokens, expert_ids, gate_weights, w_gate, w_up, w_down):
    toks, width = tokens.shape
    ff = w_gate.shape[2]
    ring = lax.axis_size("grp")
    blocks = lax.axis_size("exp")
    assert blocks == 2 * ring
    experts = ring * blocks
    rows1, rows2 = ring * toks, blocks * blocks
    cols = width // STREAMS
    vmem = pl.BlockSpec(memory_space=pltpu.VMEM)
    hbm = pl.BlockSpec(memory_space=pl.ANY)
    wide = pltpu.VMEM((STREAMS, blocks, blocks, cols), BF16)
    narrow = pltpu.VMEM((STREAMS, ring, toks, cols), BF16)
    sems = pltpu.SemaphoreType.DMA((STREAMS,))
    return pl.pallas_call(
        functools.partial(kernel, ring),
        out_shape=jax.ShapeDtypeStruct((toks, width), F32),
        in_specs=[vmem, vmem, vmem, hbm, hbm, hbm],
        out_specs=vmem,
        scratch_shapes=[
            pltpu.VMEM((toks, experts), BF16),
            pltpu.VMEM((2, ring, toks, experts), BF16),
            pltpu.VMEM((2, rows1, rows2), BF16),
            pltpu.VMEM((2, rows2, rows1), BF16),
            narrow, wide, wide, wide, wide, narrow, narrow,
            pltpu.VMEM((width, ff), BF16),
            pltpu.VMEM((width, ff), BF16),
            pltpu.VMEM((ff, width), BF16),
            pltpu.VMEM((rows2, ff), F32),
            pltpu.VMEM((rows2, ff), F32),
            pltpu.VMEM((2, rows2, ff), BF16),
            pltpu.SemaphoreType.DMA((3,)),
            pltpu.SemaphoreType.DMA((2,)),
            pltpu.SemaphoreType.DMA((2,)),
            sems, sems, sems, sems, sems, sems, sems, sems,
        ],
        compiler_params=pltpu.CompilerParams(
            collective_id=0, has_side_effects=True, vmem_limit_bytes=48 * 1024 * 1024
        ),
    )(expert_ids, gate_weights, tokens, w_gate[0], w_up[0], w_down[0])


def solution(mesh):
    return jax.shard_map(
        shards,
        mesh=mesh,
        in_specs=(
            P(("rep", "grp", "exp"), None),
            P(("rep", "grp", "exp"), None),
            P(("rep", "grp", "exp"), None),
            P(("grp", "exp"), None, None),
            P(("grp", "exp"), None, None),
            P(("grp", "exp"), None, None),
        ),
        out_specs=P(("rep", "grp", "exp"), None),
        check_vma=False,
    )
```

time: 157 us -> 70.9 us (0.45)
  Pallas kernels: 0 us -> 65.8 us
  blocking collectives: 56 us -> 0 us
  waiting for transfers between devices: 39.7 us -> 0 us
  starting transfers between devices: 35.1 us -> 0 us
  matrix products: 14.7 us -> 0 us
  local copies, waits for them, and re-layouts: 9.61 us -> 4.9 us
    pallas_call x0 -> x1, Pallas kernels: none -> 65.8 us  [shards(): pl.pallas_call(functools.partial(kernel, ring), out_shape=jax.ShapeDtypeS...]
    all_to_all x2 -> x0, blocking collectives: 56 us -> none  [the longest x1 31.8 us: shards(): lax.all_to_all(computed, 'exp', split_axis=0, concat_axis=1, tiled=True)]
    all_to_all x4 -> x0, waiting for transfers between devices: 39.7 us -> none  [the longest x1 27 us: shards(): lax.all_to_all(buffer, 'exp', split_axis=1, concat_axis=0, tiled=True)]
    all_to_all x4 -> x0, starting transfers between devices: 35.1 us -> none  [the longest x1 17.2 us: shards(): lax.all_to_all(sent_slots, 'grp', split_axis=0, concat_axis=0, tiled=True)]
    dot_general x8 -> x0, matrix products: 14.7 us -> none  [the longest x1 5.55 us: expert_apply(): jnp.dot(hidden, down_mat, preferred_element_type=jnp.float32)]
    reshape x4 -> x0, local copies, waits for them, and re-layouts: 4.96 us -> none  [the longest x1 2.54 us: shards(): computed = result.reshape(layout)]
    unnamed x7, local copies, waits for them, and re-layouts: 1.67 us -> 4.9 us
    convert_element_type x2 -> x0, local copies, waits for them, and re-layouts: 2.15 us -> none  [the longest x1 2.07 us: shards(): buffer = jnp.einsum('gesc,gcd->gesd', spread.astype(jnp.bfloat16), arrive...]
  transfers between devices with their start and end apart: 4 -> 0, of which waited for: 3 -> 0; matrix products, arithmetic and copies ran while one was open for 12% -> 0% of each run, Pallas kernels for 0% -> 0%
where the time goes in v1:
time: 70.9 us; the launch traced here: 70.7 us
  Pallas kernels  65.8 us (93%)
  local copies, waits for them, and re-layouts  4.9 us (7%)
    pallas_call x1, Pallas kernels, shards(): pl.pallas_call(functools.partial(kernel, ring), out_shape=jax.ShapeDtypeS...  65.8 us
    unnamed x7, local copies, waits for them, and re-layouts  4.9 us

profile of v1, /device:TPU:1, one launch (start us, length us, event | category | flops | bytes accessed | tf_op | source)
XLA Modules:
  0.0 70.7 jit_solution(11958151910626576602)
XLA Ops:
  0.0 0.8 %copy.8.gates_ref = bf16[16,8]{1,0:T(8,128)(2,1)S(1)} copy(bf16[16,8]{0,1:T(8,128)(2,1)} %param.8) | data formatting | bytes 512 | tf_op args[2]
  0.8 0.8 %copy.7.ids_ref = s32[16,8]{1,0:T(8,128)S(1)} copy(s32[16,8]{0,1:T(8,128)} %param.7) | data formatting | bytes 1024 | tf_op args[1]
  1.5 0.0 copy-start
  1.5 1.9 %copy-done = bf16[1,2048,768]{2,1,0:T(8,128)(2,1)S(1)} copy-done((bf16[1,2048,768]{2,1,0:T(8,128)(2,1)S(1)}, bf16[1,2048,768]{2,1,0:T(8,128)(2,1)}, u32[]{:S(2)}) %copy-start) | copy-done | bytes 3145752
  3.4 0.0 copy-start.1
  3.4 0.8 %copy-done.1 = bf16[16,2048]{1,0:T(8,128)(2,1)S(1)} copy-done((bf16[16,2048]{1,0:T(8,128)(2,1)S(1)}, bf16[16,2048]{1,0:T(8,128)(2,1)}, u32[]{:S(2)}) %copy-start.1) | copy-done | bytes 65560
  4.2 65.8 %shard_map.64 = f32[16,2048]{1,0:T(8,128)S(1)} custom-call(s32[16,8]{1,0:T(8,128)S(1)} %copy.7.ids_ref, bf16[16,8]{1,0:T(8,128)(2,1)S(1)} %copy.8.gates_ref, bf16[16,2048]{1,0:T(8,128)(2,1)S(1)} %copy-done.1, bf16[2048,768]{1,0:T(8,128)(2,1)S(1)} %bitcast.3, bf16[2048,768]{1,0:T(8,128)(2,1)} %bitcast.4, bf16[768,2048]{1,0:T(8,128)(2,1)} %bitcast.5), custom_call_target="tpu_custom_call" | custom-call | tf_op jit(solution)/shard_map/pallas_call | solution.py:287
  70.0 0.7 copy.10
Async XLA Ops:
  1.5 1.9 %copy-start = (bf16[1,2048,768]{2,1,0:T(8,128)(2,1)S(1)}, bf16[1,2048,768]{2,1,0:T(8,128)(2,1)}, u32[]{:S(2)}) copy-start(bf16[1,2048,768]{2,1,0:T(8,128)(2,1)} %param.9) | copy-start | bytes 9437188
  3.4 0.8 %copy-start.1 = (bf16[16,2048]{1,0:T(8,128)(2,1)S(1)}, bf16[16,2048]{1,0:T(8,128)(2,1)}, u32[]{:S(2)}) copy-start(bf16[16,2048]{1,0:T(8,128)(2,1)} %tok_ref.1) | copy-start | bytes 196612

commit v2 on v1

v2 whole, which is shorter than its diff:
```python
import functools
import jax
import jax.numpy as jnp
from jax import lax
from jax.experimental import pallas as pl
from jax.experimental.pallas import tpu as pltpu
from jax.sharding import PartitionSpec as P

F32 = jnp.float32
BF16 = jnp.bfloat16
STREAMS = 4
SLOTS = 2
TILE = 256
VMEM_BYTES = 67043328


def iota(shape, dim):
    return lax.broadcasted_iota(jnp.int32, shape, dim)


def dot(a, b):
    return jnp.dot(a, b, preferred_element_type=F32)


def dot_nt(a, b):
    return lax.dot_general(a, b, (((1,), (1,)), ((), ())), preferred_element_type=F32)


def kernel(
    ring,
    ids_hbm, gates_hbm, tok_hbm, wg_hbm, wu_hbm, wd_hbm, o_ref,
    ids_ref, gates_ref, tok_ref, g_own, g_in, c_tab, s_tab, in1, out2, in2, out3, in3, out4, in4,
    wg, wu, wd, acc_g, acc_u, hid,
    x_sem, w_sem, g_send, g_recv, send1, recv1, send2, recv2, send3, recv3, send4, recv4,
):
    toks, width = tok_hbm.shape
    ff = wg.shape[1]
    blocks = 2 * ring
    rows2 = blocks * ring
    rows1 = ring * toks
    experts = ring * blocks
    cols = width // STREAMS
    z = lax.axis_index("grp")
    e = lax.axis_index("exp")
    y = lax.div(e, 2)
    c = lax.rem(e, 2)

    def path_of(s):
        return s % 2

    order = [ring // 2 + ((j + 1) // 2) * (1 - 2 * (j % 2)) for j in range(ring - 1)]
    zs = {d: lax.rem(z + d, ring) for d in order}
    ys = {d: lax.rem(y + d, ring) * 2 for d in order}
    flip = 1 - c
    near_me = (z, y)
    far_me = (e, z * 2 + c)
    near = (
        [(zs[d], {"grp": zs[d], "exp": e}) for d in order],
        [(lax.div(ys[d], 2), {"grp": z, "exp": ys[d] + c}) for d in order],
    )
    far = (
        [(ys[d] + k, {"grp": z, "exp": ys[d] + k}) for d in order for k in (c, flip)]
        + [(y * 2 + flip, {"grp": z, "exp": y * 2 + flip})],
        [(zs[d] * 2 + k, {"grp": zs[d], "exp": y * 2 + k}) for d in order for k in (c, flip)]
        + [(z * 2 + flip, {"grp": z, "exp": y * 2 + flip})],
    )

    def remote(src, dst, send, recv, device):
        return pltpu.make_async_remote_copy(
            src_ref=src, dst_ref=dst, send_sem=send, recv_sem=recv,
            device_id=device, device_id_type=pl.DeviceIdType.MESH,
        )

    def wait_bytes(ref, count, sem):
        part = ref.at[pl.ds(0, count)]
        pltpu.make_async_copy(part, part, sem).wait()

    inputs = [
        pltpu.make_async_copy(hbm, vmem, x_sem.at[i])
        for i, (hbm, vmem) in enumerate(
            ((ids_hbm, ids_ref), (gates_hbm, gates_ref), (tok_hbm, tok_ref))
        )
    ]
    for copy in inputs:
        copy.start()

    barrier = pltpu.get_barrier_semaphore()

    for _, device in far[0] + far[1][:-1]:
        pl.semaphore_signal(
            barrier, inc=1, device_id=device, device_id_type=pl.DeviceIdType.MESH
        )

    inputs[0].wait()
    inputs[1].wait()
    table = jnp.zeros((experts, toks), F32)
    expert = iota((experts, toks), 0)
    for k in range(ids_ref.shape[0]):
        table = table + jnp.where(
            ids_ref[k:k + 1, :] == expert, gates_ref[k:k + 1, :].astype(F32), 0.0
        )
    same = jnp.where(iota((toks, toks), 0) == iota((toks, toks), 1), 1.0, 0.0).astype(BF16)
    table = dot_nt(same, table.astype(BF16)).astype(BF16)
    g_own[...] = table
    for path in range(2):
        g_in[path, near_me[path]] = table
    inputs[2].wait()

    pl.semaphore_wait(barrier, 4 * (ring - 1) + 1)

    for path in range(2):
        for _, device in near[path]:
            remote(
                g_own, g_in.at[path, near_me[path]], g_send.at[path], g_recv.at[path], device
            ).start()
    for s in range(STREAMS):
        path = path_of(s)
        for _, device in near[path]:
            remote(
                tok_ref.at[:, pl.ds(s * cols, cols)], in1.at[s, near_me[path]],
                send1.at[s], recv1.at[s], device,
            ).start()

    loads = [
        pltpu.make_async_copy(hbm, vmem, w_sem.at[i])
        for i, (hbm, vmem) in enumerate(((wg_hbm, wg), (wu_hbm, wu), (wd_hbm, wd)))
    ]
    for load in loads:
        load.start()
    for s in range(STREAMS):
        in1[s, near_me[path_of(s)]] = tok_ref[:, s * cols:(s + 1) * cols]

    for path in range(2):
        wait_bytes(g_in.at[path], ring - 1, g_recv.at[path])
        gates = g_in[path].reshape(rows1, experts)
        named = jnp.where(gates.astype(F32) > 0, 1.0, 0.0).astype(BF16)
        r, q = iota((rows1, rows1), 0), iota((rows1, rows1), 1)
        below = jnp.where((r // toks == q // toks) & (q < r), 1.0, 0.0).astype(BF16)
        rank = dot(below, named).astype(BF16)

        def expert_of(place, path=path):
            block = place // ring
            if path == 0:
                return z * blocks + block
            return (block // 2) * blocks + y * 2 + lax.rem(block, 2)

        pick = jnp.where(
            iota((experts, rows2), 0) == expert_of(iota((experts, rows2), 1)), 1.0, 0.0
        ).astype(BF16)
        own = iota((rows1, rows2), 0) // toks == lax.rem(iota((rows1, rows2), 1), ring)
        value, place = dot(gates, pick), dot(rank, pick)
        for b in range(SLOTS):
            c_tab[path, b] = jnp.where(own & (place == b), value, 0.0).astype(BF16)
        pick = jnp.where(
            iota((rows2, experts), 1) == expert_of(iota((rows2, experts), 0)), 1.0, 0.0
        ).astype(BF16)
        own = iota((rows2, rows1), 1) // toks == lax.rem(iota((rows2, rows1), 0), ring)
        own = own & (dot_nt(pick, gates) > 0)
        place = dot_nt(pick, rank)
        for b in range(SLOTS):
            s_tab[path, b] = jnp.where(own & (place == b), 1.0, 0.0).astype(BF16)

    for b in range(SLOTS):
        for s in range(STREAMS):
            path, n = path_of(s), b * STREAMS + s
            if b == 0:
                wait_bytes(in1.at[s], ring - 1, recv1.at[s])
            chosen = dot(s_tab[path, b], in1[s].reshape(rows1, cols)).astype(BF16)
            out2[n] = chosen.reshape(blocks, ring, cols)
            in2[n, far_me[path]] = out2[n, far_me[path]]

            for to, device in far[path]:
                remote(
                    out2.at[n, to], in2.at[n, far_me[path]], send2.at[n], recv2.at[n], device
                ).start()

    r, q = iota((rows2, rows2), 0), iota((rows2, rows2), 1)
    swapped = (
        lax.rem(r, ring) * blocks + lax.rem(r // ring, 2) * ring + r // blocks
    )
    swap = jnp.where(q == swapped, 1.0, 0.0).astype(BF16)

    for b in range(SLOTS):
        for s in range(STREAMS):
            n = b * STREAMS + s
            wait_bytes(in2.at[n], blocks - 1, recv2.at[n])
            rows = in2[n].reshape(rows2, cols)
            if path_of(s) == 1:
                rows = dot(swap, rows).astype(BF16)
            if n == 0:
                loads[0].wait()
                loads[1].wait()

            def project(j, x, s=s, rows=rows):
                at = pl.ds(pl.multiple_of(j * TILE, TILE), TILE)
                gate_part = dot(rows, wg[s * cols:(s + 1) * cols, at])
                up_part = dot(rows, wu[s * cols:(s + 1) * cols, at])
                if s > 0:
                    gate_part = gate_part + acc_g[:, at]
                    up_part = up_part + acc_u[:, at]
                if s < STREAMS - 1:
                    acc_g[:, at] = gate_part
                    acc_u[:, at] = up_part
                else:
                    hid[0, :, at] = (
                        gate_part * jax.nn.sigmoid(gate_part) * up_part
                    ).astype(BF16)
                return x
            lax.fori_loop(0, ff // TILE, project, 0)
        hid[1] = dot(swap, hid[0]).astype(BF16)
        if b == 0:
            loads[2].wait()

        for s in range(STREAMS):
            path, n = path_of(s), b * STREAMS + s
            hidden = hid[path]

            def down(j, x, s=s, n=n, hidden=hidden):
                at = pl.ds(pl.multiple_of(j * TILE, TILE), TILE)
                here = pl.ds(pl.multiple_of(s * cols + j * TILE, TILE), TILE)
                out3[n, :, :, at] = dot(hidden, wd[:, here]).astype(BF16).reshape(
                    blocks, ring, TILE
                )
                return x
            lax.fori_loop(0, cols // TILE, down, 0)
            in3[n, far_me[path]] = out3[n, far_me[path]]

            for to, device in far[path]:
                remote(
                    out3.at[n, to], in3.at[n, far_me[path]], send3.at[n], recv3.at[n], device
                ).start()

    for s in range(STREAMS):
        path = path_of(s)
        summed = jnp.zeros((rows1, cols), F32)
        for b in range(SLOTS):
            n = b * STREAMS + s
            wait_bytes(in3.at[n], blocks - 1, recv3.at[n])
            summed = summed + dot(c_tab[path, b], in3[n].reshape(rows2, cols))
        out4[s] = summed.astype(BF16).reshape(ring, toks, cols)
        in4[s, near_me[path]] = out4[s, near_me[path]]

        for to, device in near[path]:
            remote(
                out4.at[s, to], in4.at[s, near_me[path]], send4.at[s], recv4.at[s], device
            ).start()

    for s in range(STREAMS):
        wait_bytes(in4.at[s], ring - 1, recv4.at[s])
        total = in4[s, 0].astype(F32)
        for i in range(1, ring):
            total = total + in4[s, i].astype(F32)
        o_ref[:, s * cols:(s + 1) * cols] = total

    for path in range(2):
        wait_bytes(g_in.at[path], ring - 1, g_send.at[path])
    for s in range(STREAMS):
        wait_bytes(in1.at[s], ring - 1, send1.at[s])
        wait_bytes(out4.at[s], ring - 1, send4.at[s])
    for n in range(SLOTS * STREAMS):
        wait_bytes(out2.at[n], blocks - 1, send2.at[n])
        wait_bytes(out3.at[n], blocks - 1, send3.at[n])


def shards(tokens, expert_ids, gate_weights, w_gate, w_up, w_down):
    toks, width = tokens.shape
    ff = w_gate.shape[2]
    ring = lax.axis_size("grp")
    blocks = lax.axis_size("exp")
    assert blocks == 2 * ring
    experts = ring * blocks
    rows1, rows2 = ring * toks, blocks * ring
    cols = width // STREAMS
    vmem = pl.BlockSpec(memory_space=pltpu.VMEM)
    hbm = pl.BlockSpec(memory_space=pl.ANY)
    wide = pltpu.VMEM((SLOTS * STREAMS, blocks, ring, cols), BF16)
    narrow = pltpu.VMEM((STREAMS, ring, toks, cols), BF16)
    sems = pltpu.SemaphoreType.DMA((STREAMS,))
    more = pltpu.SemaphoreType.DMA((SLOTS * STREAMS,))
    return pl.pallas_call(
        functools.partial(kernel, ring),
        out_shape=jax.ShapeDtypeStruct((toks, width), F32),
        in_specs=[hbm] * 6,
        out_specs=vmem,
        scratch_shapes=[
            pltpu.VMEM(expert_ids.shape[::-1], jnp.int32),
            pltpu.VMEM(expert_ids.shape[::-1], BF16),
            pltpu.VMEM((toks, width), BF16),
            pltpu.VMEM((toks, experts), BF16),
            pltpu.VMEM((2, ring, toks, experts), BF16),
            pltpu.VMEM((2, SLOTS, rows1, rows2), BF16),
            pltpu.VMEM((2, SLOTS, rows2, rows1), BF16),
            narrow, wide, wide, wide, wide, narrow, narrow,
            pltpu.VMEM((width, ff), BF16),
            pltpu.VMEM((width, ff), BF16),
            pltpu.VMEM((ff, width), BF16),
            pltpu.VMEM((rows2, ff), F32),
            pltpu.VMEM((rows2, ff), F32),
            pltpu.VMEM((2, rows2, ff), BF16),
            pltpu.SemaphoreType.DMA((3,)),
            pltpu.SemaphoreType.DMA((3,)),
            pltpu.SemaphoreType.DMA((2,)),
            pltpu.SemaphoreType.DMA((2,)),
            sems, sems, more, more, more, more, sems, sems,
        ],
        compiler_params=pltpu.CompilerParams(
            collective_id=0, has_side_effects=True, vmem_limit_bytes=VMEM_BYTES
        ),
    )(expert_ids.T, gate_weights.T, tokens, w_gate[0], w_up[0], w_down[0])


def solution(mesh):
    return jax.shard_map(
        shards,
        mesh=mesh,
        in_specs=(
            P(("rep", "grp", "exp"), None),
            P(("rep", "grp", "exp"), None),
            P(("rep", "grp", "exp"), None),
            P(("grp", "exp"), None, None),
            P(("grp", "exp"), None, None),
            P(("grp", "exp"), None, None),
        ),
        out_specs=P(("rep", "grp", "exp"), None),
        check_vma=False,
    )
```

time: 70.9 us -> 62.6 us (0.88)
  Pallas kernels: 65.8 us -> 60.8 us
  local copies, waits for them, and re-layouts: 4.9 us -> 1.57 us
    pallas_call x1, Pallas kernels: 65.8 us -> 60.8 us  [shards(): pl.pallas_call(functools.partial(kernel, ring), out_shape=jax.ShapeDtypeS...]
    unnamed x7 -> x1, local copies, waits for them, and re-layouts: 4.9 us -> 1.57 us
where the time goes in v2:
time: 62.6 us; the launch traced here: 62.4 us
  Pallas kernels  60.8 us (97%)
  local copies, waits for them, and re-layouts  1.57 us (3%)
    pallas_call x1, Pallas kernels, shards(): pl.pallas_call(functools.partial(kernel, ring), out_shape=jax.ShapeDtypeS...  60.8 us
    unnamed x1, local copies, waits for them, and re-layouts  1.57 us

profile of v2, /device:TPU:1, one launch (start us, length us, event | category | flops | bytes accessed | tf_op | source)
XLA Modules:
  0.0 62.4 jit_solution(912690739970340060)
XLA Ops:
  0.0 60.8 %shard_map.64 = f32[16,2048]{1,0:T(8,128)} custom-call(s32[8,16]{1,0:T(8,128)} %bitcast.8, bf16[8,16]{1,0:T(8,128)(2,1)} %bitcast.9, bf16[16,2048]{1,0:T(8,128)(2,1)} %tok_hbm.1, bf16[2048,768]{1,0:T(8,128)(2,1)} %bitcast.5, bf16[2048,768]{1,0:T(8,128)(2,1)} %bitcast.6, bf16[768,2048]{1,0:T(8,128)(2,1)} %bitcast.7), custom_call_target="tpu_custom_call" | custom-call | tf_op jit(solution)/shard_map/pallas_call | solution.py:280
  60.8 1.6 %copy.8 = f32[16,2048]{1,0:T(8,128)} copy(f32[16,2048]{1,0:T(8,128)} %shard_map.64) | data formatting | bytes 262144

commit v3 on v2

--- a/solution.py
+++ b/solution.py
@@ -8,10 +8,11 @@
 
 F32 = jnp.float32
 BF16 = jnp.bfloat16
-STREAMS = 4
+CUTS = (512,)
+BACK = 1
 SLOTS = 2
 TILE = 256
-VMEM_BYTES = 67043328
+VMEM_BYTES = 48 * 1024 * 1024
 
 
 def iota(shape, dim):
@@ -39,14 +40,21 @@
     rows2 = blocks * ring
     rows1 = ring * toks
     experts = ring * blocks
-    cols = width // STREAMS
     z = lax.axis_index("grp")
     e = lax.axis_index("exp")
     y = lax.div(e, 2)
     c = lax.rem(e, 2)
 
-    def path_of(s):
-        return s % 2
+    half = width // 2
+    edges = (0,) + CUTS + (half,)
+    out_chunks = [
+        (path, left, right - left) for left, right in zip(edges, edges[1:]) for path in range(2)
+    ]
+    back_chunks = [
+        (path, left, size)
+        for _, left, size in out_chunks[::2][::BACK] for path in range(2)
+    ]
+    chunks = len(out_chunks)
 
     order = [ring // 2 + ((j + 1) // 2) * (1 - 2 * (j % 2)) for j in range(ring - 1)]
     zs = {d: lax.rem(z + d, ring) for d in order}
@@ -113,12 +121,15 @@
             remote(
                 g_own, g_in.at[path, near_me[path]], g_send.at[path], g_recv.at[path], device
             ).start()
-    for s in range(STREAMS):
-        path = path_of(s)
+    def block(path, source, start, size):
+        return in1.at[path, source, :, pl.ds(start, size)]
+
+    for n, (path, start, size) in enumerate(out_chunks):
         for _, device in near[path]:
             remote(
-                tok_ref.at[:, pl.ds(s * cols, cols)], in1.at[s, near_me[path]],
-                send1.at[s], recv1.at[s], device,
+                tok_ref.at[:, pl.ds(path * half + start, size)],
+                block(path, near_me[path], start, size),
+                send1.at[n], recv1.at[n], device,
             ).start()
 
     loads = [
@@ -127,8 +138,8 @@
     ]
     for load in loads:
         load.start()
-    for s in range(STREAMS):
-        in1[s, near_me[path_of(s)]] = tok_ref[:, s * cols:(s + 1) * cols]
+    for path in range(2):
+        in1[path, near_me[path]] = tok_ref[:, path * half:(path + 1) * half]
 
     for path in range(2):
         wait_bytes(g_in.at[path], ring - 1, g_recv.at[path])
@@ -161,17 +172,20 @@
             s_tab[path, b] = jnp.where(own & (place == b), 1.0, 0.0).astype(BF16)
 
     for b in range(SLOTS):
-        for s in range(STREAMS):
-            path, n = path_of(s), b * STREAMS + s
+        for i, (path, start, size) in enumerate(out_chunks):
+            n = b * chunks + i
+            at = slice(start, start + size)
             if b == 0:
-                wait_bytes(in1.at[s], ring - 1, recv1.at[s])
-            chosen = dot(s_tab[path, b], in1[s].reshape(rows1, cols)).astype(BF16)
-            out2[n] = chosen.reshape(blocks, ring, cols)
-            in2[n, far_me[path]] = out2[n, far_me[path]]
-
+                wait_bytes(in1.at[path, :, :, pl.ds(start, size)], ring - 1, recv1.at[i])
+            rows = in1[path, :, :, at].reshape(rows1, size)
+            chosen = dot(s_tab[path, b], rows).astype(BF16)
+            out2[b, path, :, :, at] = chosen.reshape(blocks, ring, size)
+            in2[b, path, far_me[path], :, at] = out2[b, path, far_me[path], :, at]
             for to, device in far[path]:
                 remote(
-                    out2.at[n, to], in2.at[n, far_me[path]], send2.at[n], recv2.at[n], device
+                    out2.at[b, path, to, :, pl.ds(start, size)],
+                    in2.at[b, path, far_me[path], :, pl.ds(start, size)],
+                    send2.at[n], recv2.at[n], device,
                 ).start()
 
     r, q = iota((rows2, rows2), 0), iota((rows2, rows2), 1)
@@ -181,24 +195,25 @@
     swap = jnp.where(q == swapped, 1.0, 0.0).astype(BF16)
 
     for b in range(SLOTS):
-        for s in range(STREAMS):
-            n = b * STREAMS + s
-            wait_bytes(in2.at[n], blocks - 1, recv2.at[n])
-            rows = in2[n].reshape(rows2, cols)
-            if path_of(s) == 1:
+        last = len(out_chunks) - 1
+        for i, (path, start, size) in enumerate(out_chunks):
+            n = b * chunks + i
+            wait_bytes(in2.at[b, path, :, :, pl.ds(start, size)], blocks - 1, recv2.at[n])
+            rows = in2[b, path, :, :, start:start + size].reshape(rows2, size)
+            if path == 1:
                 rows = dot(swap, rows).astype(BF16)
             if n == 0:
                 loads[0].wait()
                 loads[1].wait()
 
-            def project(j, x, s=s, rows=rows):
+            def project(j, x, i=i, rows=rows, top=path * half + start, size=size, last=last):
                 at = pl.ds(pl.multiple_of(j * TILE, TILE), TILE)
-                gate_part = dot(rows, wg[s * cols:(s + 1) * cols, at])
-                up_part = dot(rows, wu[s * cols:(s + 1) * cols, at])
-                if s > 0:
+                gate_part = dot(rows, wg[top:top + size, at])
+                up_part = dot(rows, wu[top:top + size, at])
+                if i > 0:
                     gate_part = gate_part + acc_g[:, at]
                     up_part = up_part + acc_u[:, at]
-                if s < STREAMS - 1:
+                if i < last:
                     acc_g[:, at] = gate_part
                     acc_u[:, at] = up_part
                 else:
@@ -211,55 +226,65 @@
         if b == 0:
             loads[2].wait()
 
-        for s in range(STREAMS):
-            path, n = path_of(s), b * STREAMS + s
+        for i, (path, start, size) in enumerate(back_chunks):
+            n = b * chunks + i
             hidden = hid[path]
 
-            def down(j, x, s=s, n=n, hidden=hidden):
-                at = pl.ds(pl.multiple_of(j * TILE, TILE), TILE)
-                here = pl.ds(pl.multiple_of(s * cols + j * TILE, TILE), TILE)
-                out3[n, :, :, at] = dot(hidden, wd[:, here]).astype(BF16).reshape(
+            def down(j, x, b=b, path=path, start=start, hidden=hidden):
+                at = pl.ds(pl.multiple_of(start + j * TILE, TILE), TILE)
+                here = pl.ds(pl.multiple_of(path * half + start + j * TILE, TILE), TILE)
+                out3[b, path, :, :, at] = dot(hidden, wd[:, here]).astype(BF16).reshape(
                     blocks, ring, TILE
                 )
                 return x
-            lax.fori_loop(0, cols // TILE, down, 0)
-            in3[n, far_me[path]] = out3[n, far_me[path]]
-
+            lax.fori_loop(0, size // TILE, down, 0)
+            at = slice(start, start + size)
+            in3[b, path, far_me[path], :, at] = out3[b, path, far_me[path], :, at]
             for to, device in far[path]:
                 remote(
-                    out3.at[n, to], in3.at[n, far_me[path]], send3.at[n], recv3.at[n], device
+                    out3.at[b, path, to, :, pl.ds(start, size)],
+                    in3.at[b, path, far_me[path], :, pl.ds(start, size)],
+                    send3.at[n], recv3.at[n], device,
                 ).start()
 
-    for s in range(STREAMS):
-        path = path_of(s)
-        summed = jnp.zeros((rows1, cols), F32)
-        for b in range(SLOTS):
-            n = b * STREAMS + s
-            wait_bytes(in3.at[n], blocks - 1, recv3.at[n])
-            summed = summed + dot(c_tab[path, b], in3[n].reshape(rows2, cols))
-        out4[s] = summed.astype(BF16).reshape(ring, toks, cols)
-        in4[s, near_me[path]] = out4[s, near_me[path]]
-
+    for n, (path, start, size) in enumerate(back_chunks):
+        summed = jnp.zeros((rows1, size), F32)
+        at = slice(start, start + size)
+        for b in range(SLOTS):
+            wait_bytes(
+                in3.at[b, path, :, :, pl.ds(start, size)], blocks - 1, recv3.at[b * chunks + n]
+            )
+            back = in3[b, path, :, :, at].reshape(rows2, size)
+            summed = summed + dot(c_tab[path, b], back)
+        out4[path, :, :, at] = summed.astype(BF16).reshape(ring, toks, size)
+        in4[path, near_me[path], :, at] = out4[path, near_me[path], :, at]
         for to, device in near[path]:
             remote(
-                out4.at[s, to], in4.at[s, near_me[path]], send4.at[s], recv4.at[s], device
+                out4.at[path, to, :, pl.ds(start, size)],
+                in4.at[path, near_me[path], :, pl.ds(start, size)],
+                send4.at[n], recv4.at[n], device,
             ).start()
 
-    for s in range(STREAMS):
-        wait_bytes(in4.at[s], ring - 1, recv4.at[s])
-        total = in4[s, 0].astype(F32)
+    for n, (path, start, size) in enumerate(back_chunks):
+        wait_bytes(in4.at[path, :, :, pl.ds(start, size)], ring - 1, recv4.at[n])
+        at = slice(start, start + size)
+        total = in4[path, 0, :, at].astype(F32)
         for i in range(1, ring):
-            total = total + in4[s, i].astype(F32)
-        o_ref[:, s * cols:(s + 1) * cols] = total
+            total = total + in4[path, i, :, at].astype(F32)
+        o_ref[:, path * half + start:path * half + start + size] = total
 
     for path in range(2):
         wait_bytes(g_in.at[path], ring - 1, g_send.at[path])
-    for s in range(STREAMS):
-        wait_bytes(in1.at[s], ring - 1, send1.at[s])
-        wait_bytes(out4.at[s], ring - 1, send4.at[s])
-    for n in range(SLOTS * STREAMS):
-        wait_bytes(out2.at[n], blocks - 1, send2.at[n])
-        wait_bytes(out3.at[n], blocks - 1, send3.at[n])
+    for n, (path, start, size) in enumerate(out_chunks):
+        wait_bytes(in1.at[path, :, :, pl.ds(start, size)], ring - 1, send1.at[n])
+        for b in range(SLOTS):
+            part = out2.at[b, path, :, :, pl.ds(start, size)]
+            wait_bytes(part, blocks - 1, send2.at[b * chunks + n])
+    for n, (path, start, size) in enumerate(back_chunks):
+        wait_bytes(out4.at[path, :, :, pl.ds(start, size)], ring - 1, send4.at[n])
+        for b in range(SLOTS):
+            part = out3.at[b, path, :, :, pl.ds(start, size)]
+            wait_bytes(part, blocks - 1, send3.at[b * chunks + n])
 
 
 def shards(tokens, expert_ids, gate_weights, w_gate, w_up, w_down):
@@ -270,13 +295,12 @@
     assert blocks == 2 * ring
     experts = ring * blocks
     rows1, rows2 = ring * toks, blocks * ring
-    cols = width // STREAMS
     vmem = pl.BlockSpec(memory_space=pltpu.VMEM)
     hbm = pl.BlockSpec(memory_space=pl.ANY)
-    wide = pltpu.VMEM((SLOTS * STREAMS, blocks, ring, cols), BF16)
-    narrow = pltpu.VMEM((STREAMS, ring, toks, cols), BF16)
-    sems = pltpu.SemaphoreType.DMA((STREAMS,))
-    more = pltpu.SemaphoreType.DMA((SLOTS * STREAMS,))
+    wide = pltpu.VMEM((SLOTS, 2, blocks, ring, width // 2), BF16)
+    narrow = pltpu.VMEM((2, ring, toks, width // 2), BF16)
+    sems = pltpu.SemaphoreType.DMA((2 * len(CUTS) + 2,))
+    more = pltpu.SemaphoreType.DMA((SLOTS * (2 * len(CUTS) + 2),))
     return pl.pallas_call(
         functools.partial(kernel, ring),
         out_shape=jax.ShapeDtypeStruct((toks, width), F32),
@@ -306,7 +330,10 @@
         compiler_params=pltpu.CompilerParams(
             collective_id=0, has_side_effects=True, vmem_limit_bytes=VMEM_BYTES
         ),
-    )(expert_ids.T, gate_weights.T, tokens, w_gate[0], w_up[0], w_down[0])
+    )(*(
+        pltpu.with_memory_space_constraint(x, pltpu.HBM)
+        for x in (expert_ids.T, gate_weights.T, tokens, w_gate[0], w_up[0], w_down[0])
+    ))
 
 
 def solution(mesh):

time: 62.6 us -> 61.1 us (0.976)
  local copies, waits for them, and re-layouts: 1.57 us -> 0.66 us
    unnamed x1, local copies, waits for them, and re-layouts: 1.57 us -> 0.66 us
where the time goes in v3:
time: 61.1 us; the launch traced here: 60.9 us
  Pallas kernels  60.2 us (99%)
  local copies, waits for them, and re-layouts  0.66 us (1%)
    pallas_call x1, Pallas kernels, shards(): pl.pallas_call(functools.partial(kernel, ring), out_shape=jax.ShapeDtypeS...  60.2 us

profile of v3, /device:TPU:1, one launch (start us, length us, event | category | flops | bytes accessed | tf_op | source)
XLA Modules:
  0.0 60.9 jit_solution(2221811800858889697)
XLA Ops:
  0.0 60.2 %shard_map.64 = f32[16,2048]{1,0:T(8,128)S(1)} custom-call(s32[8,16]{1,0:T(8,128)} %bitcast.8, bf16[8,16]{1,0:T(8,128)(2,1)} %bitcast.9, bf16[16,2048]{1,0:T(8,128)(2,1)} %tok_hbm.1, bf16[2048,768]{1,0:T(8,128)(2,1)} %bitcast.5, bf16[2048,768]{1,0:T(8,128)(2,1)} %bitcast.6, bf16[768,2048]{1,0:T(8,128)(2,1)} %bitcast.7), custom_call_target="tpu_custom_call" | custom-call | tf_op jit(solution)/shard_map/pallas_call | solution.py:304
  60.2 0.7 %copy.8 = f32[16,2048]{1,0:T(8,128)} copy(f32[16,2048]{1,0:T(8,128)S(1)} %shard_map.64) | data formatting | bytes 262144

commit v4 on v3

--- a/solution.py
+++ b/solution.py
@@ -31,7 +31,7 @@
     ring,
     ids_hbm, gates_hbm, tok_hbm, wg_hbm, wu_hbm, wd_hbm, o_ref,
     ids_ref, gates_ref, tok_ref, g_own, g_in, c_tab, s_tab, in1, out2, in2, out3, in3, out4, in4,
-    wg, wu, wd, acc_g, acc_u, hid,
+    wg, wu, wd, acc_g, acc_u, hid, sums,
     x_sem, w_sem, g_send, g_recv, send1, recv1, send2, recv2, send3, recv3, send4, recv4,
 ):
     toks, width = tok_hbm.shape
@@ -247,15 +247,17 @@
                     send3.at[n], recv3.at[n], device,
                 ).start()
 
+    def weigh(b, n, path, start, size):
+        part = in3.at[b, path, :, :, pl.ds(start, size)]
+        wait_bytes(part, blocks - 1, recv3.at[b * chunks + n])
+        back = in3[b, path, :, :, start:start + size].reshape(rows2, size)
+        return dot(c_tab[path, b], back)
+
     for n, (path, start, size) in enumerate(back_chunks):
-        summed = jnp.zeros((rows1, size), F32)
+        sums[path, :, start:start + size] = weigh(0, n, path, start, size)
+    for n, (path, start, size) in enumerate(back_chunks):
         at = slice(start, start + size)
-        for b in range(SLOTS):
-            wait_bytes(
-                in3.at[b, path, :, :, pl.ds(start, size)], blocks - 1, recv3.at[b * chunks + n]
-            )
-            back = in3[b, path, :, :, at].reshape(rows2, size)
-            summed = summed + dot(c_tab[path, b], back)
+        summed = sums[path, :, at] + weigh(1, n, path, start, size)
         out4[path, :, :, at] = summed.astype(BF16).reshape(ring, toks, size)
         in4[path, near_me[path], :, at] = out4[path, near_me[path], :, at]
         for to, device in near[path]:
@@ -321,6 +323,7 @@
             pltpu.VMEM((rows2, ff), F32),
             pltpu.VMEM((rows2, ff), F32),
             pltpu.VMEM((2, rows2, ff), BF16),
+            pltpu.VMEM((2, rows1, width // 2), F32),
             pltpu.SemaphoreType.DMA((3,)),
             pltpu.SemaphoreType.DMA((3,)),
             pltpu.SemaphoreType.DMA((2,)),

time: 61.1 us -> 61 us (level)
  no operation moved by 1% of the time
where the time goes in v4:
time: 61 us; the launch traced here: 60.9 us
  Pallas kernels  60.2 us (99%)
  local copies, waits for them, and re-layouts  0.66 us (1%)
    pallas_call x1, Pallas kernels, shards(): pl.pallas_call(functools.partial(kernel, ring), out_shape=jax.ShapeDtypeS...  60.2 us

profile of v4, /device:TPU:1, one launch (start us, length us, event | category | flops | bytes accessed | tf_op | source)
XLA Modules:
  0.0 60.9 jit_solution(10112028998869014353)
XLA Ops:
  0.0 60.2 %shard_map.64 = f32[16,2048]{1,0:T(8,128)S(1)} custom-call(s32[8,16]{1,0:T(8,128)} %bitcast.8, bf16[8,16]{1,0:T(8,128)(2,1)} %bitcast.9, bf16[16,2048]{1,0:T(8,128)(2,1)} %tok_hbm.1, bf16[2048,768]{1,0:T(8,128)(2,1)} %bitcast.5, bf16[2048,768]{1,0:T(8,128)(2,1)} %bitcast.6, bf16[768,2048]{1,0:T(8,128)(2,1)} %bitcast.7), custom_call_target="tpu_custom_call" | custom-call | tf_op jit(solution)/shard_map/pallas_call | solution.py:306
  60.2 0.7 %copy.8 = f32[16,2048]{1,0:T(8,128)} copy(f32[16,2048]{1,0:T(8,128)S(1)} %shard_map.64) | data formatting | bytes 262144

commit v5 on v4

--- a/solution.py
+++ b/solution.py
@@ -141,6 +141,13 @@
     for path in range(2):
         in1[path, near_me[path]] = tok_ref[:, path * half:(path + 1) * half]
 
+    def expert_of(path, place):
+        block = place // ring
+        if path == 0:
+            return z * blocks + block
+        return (block // 2) * blocks + y * 2 + lax.rem(block, 2)
+
+    ranks = []
     for path in range(2):
         wait_bytes(g_in.at[path], ring - 1, g_recv.at[path])
         gates = g_in[path].reshape(rows1, experts)
@@ -148,22 +155,9 @@
         r, q = iota((rows1, rows1), 0), iota((rows1, rows1), 1)
         below = jnp.where((r // toks == q // toks) & (q < r), 1.0, 0.0).astype(BF16)
         rank = dot(below, named).astype(BF16)
-
-        def expert_of(place, path=path):
-            block = place // ring
-            if path == 0:
-                return z * blocks + block
-            return (block // 2) * blocks + y * 2 + lax.rem(block, 2)
-
+        ranks.append(rank)
         pick = jnp.where(
-            iota((experts, rows2), 0) == expert_of(iota((experts, rows2), 1)), 1.0, 0.0
-        ).astype(BF16)
-        own = iota((rows1, rows2), 0) // toks == lax.rem(iota((rows1, rows2), 1), ring)
-        value, place = dot(gates, pick), dot(rank, pick)
-        for b in range(SLOTS):
-            c_tab[path, b] = jnp.where(own & (place == b), value, 0.0).astype(BF16)
-        pick = jnp.where(
-            iota((rows2, experts), 1) == expert_of(iota((rows2, experts), 0)), 1.0, 0.0
+            iota((rows2, experts), 1) == expert_of(path, iota((rows2, experts), 0)), 1.0, 0.0
         ).astype(BF16)
         own = iota((rows2, rows1), 1) // toks == lax.rem(iota((rows2, rows1), 0), ring)
         own = own & (dot_nt(pick, gates) > 0)
@@ -187,6 +181,17 @@
                     in2.at[b, path, far_me[path], :, pl.ds(start, size)],
                     send2.at[n], recv2.at[n], device,
                 ).start()
+
+    for path in range(2):
+        gates = g_in[path].reshape(rows1, experts)
+        rank = ranks[path]
+        pick = jnp.where(
+            iota((experts, rows2), 0) == expert_of(path, iota((experts, rows2), 1)), 1.0, 0.0
+        ).astype(BF16)
+        own = iota((rows1, rows2), 0) // toks == lax.rem(iota((rows1, rows2), 1), ring)
+        value, place = dot(gates, pick), dot(rank, pick)
+        for b in range(SLOTS):
+            c_tab[path, b] = jnp.where(own & (place == b), value, 0.0).astype(BF16)
 
     r, q = iota((rows2, rows2), 0), iota((rows2, rows2), 1)
     swapped = (

time: 61 us -> 61 us (level)
  no operation moved by 1% of the time
where the time goes in v5:
time: 61 us; the launch traced here: 60.8 us
  Pallas kernels  60.1 us (99%)
  local copies, waits for them, and re-layouts  0.66 us (1%)
    pallas_call x1, Pallas kernels, shards(): pl.pallas_call(functools.partial(kernel, ring), out_shape=jax.ShapeDtypeS...  60.1 us

profile of v5, /device:TPU:1, one launch (start us, length us, event | category | flops | bytes accessed | tf_op | source)
XLA Modules:
  0.0 60.8 jit_solution(18322955899326298524)
XLA Ops:
  0.0 60.1 %shard_map.64 = f32[16,2048]{1,0:T(8,128)S(1)} custom-call(s32[8,16]{1,0:T(8,128)} %bitcast.8, bf16[8,16]{1,0:T(8,128)(2,1)} %bitcast.9, bf16[16,2048]{1,0:T(8,128)(2,1)} %tok_hbm.1, bf16[2048,768]{1,0:T(8,128)(2,1)} %bitcast.5, bf16[2048,768]{1,0:T(8,128)(2,1)} %bitcast.6, bf16[768,2048]{1,0:T(8,128)(2,1)} %bitcast.7), custom_call_target="tpu_custom_call" | custom-call | tf_op jit(solution)/shard_map/pallas_call | solution.py:311
  60.1 0.7 %copy.8 = f32[16,2048]{1,0:T(8,128)} copy(f32[16,2048]{1,0:T(8,128)S(1)} %shard_map.64) | data formatting | bytes 262144
